TPU v7x, 32 devices: a whole 2x2x4 slice. The times are simulated.
32 devices in a mesh: twin: 2 (over y), gx: 4 (over z), gy: 2 (over core), gz: 2 (over x).
Axes of the slice: x: 2, y: 2, z: 4, core: 2. Of those that a mesh axis runs over, the one named last changes fastest.
Arguments:
- potential: float32 [64, 32, 256], P(('twin', 'gx'), 'gy', 'gz'), parts along dimension 0, may hold values from 0 to 1
- gating: float32 [64, 32, 256], P(('twin', 'gx'), 'gy', 'gz'), parts along dimension 0, may hold values from 0 to 1
- adjoint_v: float32 [64, 32, 256], P(('twin', 'gx'), 'gy', 'gz'), parts along dimension 0, may hold values from -6 to 6
- adjoint_h: float32 [64, 32, 256], P(('twin', 'gx'), 'gy', 'gz'), parts along dimension 0, may hold values from -6 to 6
- recorded: float32 [64, 32, 256], P(('twin', 'gx'), 'gy', 'gz'), parts along dimension 0, may hold values from 0 to 1
- tissue_mask: int32 [64, 32, 256], P(('twin', 'gx'), 'gy', 'gz'), parts along dimension 0, may hold values from 0 to 1
- fibre_sector: int32 [64, 32, 256], P(('twin', 'gx'), 'gy', 'gz'), parts along dimension 0, may hold values from 0 to 11
- region_label: int32 [64, 32, 256], P(('twin', 'gx'), 'gy', 'gz'), parts along dimension 0, may hold values from 0 to 15
- fibre_table: float32 [24, 9], P('twin'), parts along dimension 0, may hold values from 0.005 to 0.025
- conductance: float32 [32], P('twin'), parts along dimension 0, may hold values from 0.5 to 2
Outputs:
- lambda_v: float32 [64, 32, 256], P(('twin', 'gx'), 'gy', 'gz'), parts along dimension 0
- lambda_h: float32 [64, 32, 256], P(('twin', 'gx'), 'gy', 'gz'), parts along dimension 0
- sensitivity: float32 [32], P('twin'), parts along dimension 0
There are 2 independent parts, one for each index of `twin`. A program takes and returns all parts, laid end to end along the dimension named above; each array names one. Nothing has to cross between parts.
All inputs are finite; a program needn't handle non-finite values.
Results may differ from a plain program's by a relative error of at most 0.0003.
Values sent between devices are 32-bit elements; how exact they have to be, the bound alone decides.
No kernel may reach another device: no remote copies, remote signals or barrier semaphores. Data moves between devices by JAX's collectives and lax.ppermute only.
A program may use at most 64 MiB of HBM per device.

v0:
```python
import math
import jax
import jax.numpy as jnp
from jax import lax
from jax.sharding import PartitionSpec as P

WINDOW_STEPS = 3
step_size = 0.1
tau_inward = 0.3
tau_outward = 6.0
tau_opening = 12.0
tau_closing = 15.0
gate_level = 0.13
gate_width = 0.02
gradient_gain = 30.0
PAIR_OFFSETS = (
    (1, 0, 0),
    (0, 1, 0),
    (0, 0, 1),
    (1, 1, 0),
    (1, -1, 0),
    (1, 0, 1),
    (1, 0, -1),
    (0, 1, 1),
    (0, 1, -1),
)


def extended(array, sides, width):
    for axis, dim in sides:
        count, length = (lax.axis_size(axis), array.shape[dim])
        up = [(i, (i + 1) % count) for i in range(count - 1)]
        down = [(j, i) for i, j in up]
        last = lax.slice_in_dim(array, length - width, length, axis=dim)
        initial = lax.slice_in_dim(array, 0, width, axis=dim)
        before = lax.ppermute(last, axis, up)
        after = lax.ppermute(initial, axis, down)
        array = jnp.concatenate([before, array, after], axis=dim)
    return array


def crop(array, trim):
    if trim == 0:
        return array
    return array[..., trim:-trim, trim:-trim, trim:-trim]


def shifted(padded, offset):
    sizes = [padded.shape[-3 + axis] - 2 for axis in range(3)]
    starts = [1 + offset[axis] for axis in range(3)]
    return padded[
        ...,
        starts[0] : starts[0] + sizes[0],
        starts[1] : starts[1] + sizes[1],
        starts[2] : starts[2] + sizes[2],
    ]


def neighbour_terms(field_pad, tissue_pad, flux_pad):
    centre = crop(field_pad, 1)
    tissue_mid = crop(tissue_pad, 1)
    flux_mid = crop(flux_pad, 1)
    total = jnp.zeros_like(centre)
    for direction, base in enumerate(PAIR_OFFSETS):
        for sign in (1, -1):
            offset = tuple((sign * part for part in base))
            coupling = 0.5 * (
                flux_mid[direction] * shifted(tissue_pad, offset)
                + shifted(flux_pad[direction], offset) * tissue_mid
            )
            total = total + coupling * (shifted(field_pad, offset) - centre)
    return total


def region_terms(adjoint_pad, field_pad, tissue_pad, fibre_mid):
    adjoint_mid = crop(adjoint_pad, 1)
    centre = crop(field_pad, 1)
    total = jnp.zeros_like(centre)
    for direction, base in enumerate(PAIR_OFFSETS):
        for sign in (1, -1):
            offset = tuple((sign * part for part in base))
            weight = shifted(tissue_pad, offset) * fibre_mid[direction]
            total = total + weight * (shifted(adjoint_pad, offset) - adjoint_mid) * (
                shifted(field_pad, offset) - centre
            )
    return -0.5 * crop(tissue_pad, 1) * total


def ionic(volts, gate_now):
    switch = jax.nn.sigmoid((volts - gate_level) / gate_width)
    drive_v = gate_now * volts * volts * (1.0 - volts) / tau_inward - volts / tau_outward
    drive_h = (1.0 - switch) * (1.0 - gate_now) / tau_opening - switch * gate_now / tau_closing
    return (drive_v, drive_h)


def ionic_partials(volts, gate_now):
    switch = jax.nn.sigmoid((volts - gate_level) / gate_width)
    slope = switch * (1.0 - switch) / gate_width
    deriv_vv = gate_now * (2.0 * volts - 3.0 * volts * volts) / tau_inward - 1.0 / tau_outward
    deriv_vh = volts * volts * (1.0 - volts) / tau_inward
    deriv_hv = slope * (-(1.0 - gate_now) / tau_opening - gate_now / tau_closing)
    deriv_hh = -(1.0 - switch) / tau_opening - switch / tau_closing
    return (deriv_vv, deriv_vh, deriv_hv, deriv_hh)


def forward_step(volts_pad, gate_now, tissue_mid, tissue_pad, flux_pad):
    volts = crop(volts_pad, 1)
    drive_v, drive_h = ionic(volts, gate_now)
    spread = neighbour_terms(volts_pad, tissue_pad, flux_pad)
    return (
        volts + tissue_mid * (spread + step_size * drive_v),
        gate_now + tissue_mid * step_size * drive_h,
    )


def local_coefficients(tissue_mask, fibre_sector, region_label, fibre_table, conductance):
    tissue_local = tissue_mask.astype(jnp.float32)
    local_factor = jnp.zeros(tissue_local.shape, jnp.float32)
    for label in range(conductance.shape[0]):
        local_factor = local_factor + jnp.where(region_label == label, conductance[label], 0.0)
    fibre_local = jnp.zeros((9,) + tissue_local.shape, jnp.float32)
    for label in range(fibre_table.shape[0]):
        fibre_local = fibre_local + jnp.where(
            (fibre_sector == label)[None], fibre_table[label][:, None, None, None], 0.0
        )
    flux_local = (tissue_local * local_factor)[None] * fibre_local
    return (tissue_local, fibre_local, flux_local)


def local(
    potential,
    gating,
    adjoint_v,
    adjoint_h,
    recorded,
    tissue_mask,
    fibre_sector,
    region_label,
    fibre_table,
    conductance,
):
    span = 1
    tissue_local, fibre_mid, flux_local = local_coefficients(
        tissue_mask, fibre_sector, region_label, fibre_table, conductance
    )
    flux_all = extended(flux_local, (("gx", 1), ("gy", 2), ("gz", 3)), span)
    tissue_all = jnp.where(flux_all[0] > 0.0, 1.0, 0.0).astype(jnp.float32)
    tissue_pad = crop(tissue_all, span - 1)
    flux_pad = crop(flux_all, span - 1)
    saved_pads = []
    saved_gates = []
    volts = potential
    gate_now = gating
    for step in range(WINDOW_STEPS):
        volts_pad = extended(volts, (("gx", 0), ("gy", 1), ("gz", 2)), 1)
        saved_pads.append(volts_pad)
        saved_gates.append(gate_now)
        volts, gate_now = forward_step(volts_pad, gate_now, tissue_local, tissue_pad, flux_pad)
    back_v = adjoint_v + tissue_local * (volts - recorded)
    back_h = adjoint_h
    region_count = conductance.shape[0]
    selector = (
        region_label[None] == jnp.arange(region_count, dtype=jnp.int32)[:, None, None, None]
    ).astype(jnp.float32)
    total = jnp.zeros((region_count,), jnp.float32)
    for step in reversed(range(WINDOW_STEPS)):
        masked = tissue_local * back_v
        masked_pad = extended(masked, (("gx", 0), ("gy", 1), ("gz", 2)), 1)
        volts_pad = saved_pads[step]
        terms = region_terms(masked_pad, volts_pad, tissue_pad, fibre_mid)
        partial_sums = jnp.einsum(
            "rxyz,xyz->r", selector, terms, precision=jax.lax.Precision.HIGHEST
        )
        total = total + lax.psum(partial_sums, ("gx", "gy", "gz"))
        deriv_vv, deriv_vh, deriv_hv, deriv_hh = ionic_partials(
            crop(volts_pad, 1), saved_gates[step]
        )
        spread = neighbour_terms(masked_pad, tissue_pad, flux_pad)
        next_v = (
            back_v + spread + step_size * tissue_local * (deriv_vv * back_v + deriv_hv * back_h)
        )
        next_h = back_h + step_size * tissue_local * (deriv_vh * back_v + deriv_hh * back_h)
        back_v, back_h = (next_v, next_h)
    cells = (
        potential.shape[0]
        * potential.shape[1]
        * potential.shape[2]
        * lax.axis_size("gx")
        * lax.axis_size("gy")
        * lax.axis_size("gz")
    )
    scale = gradient_gain / math.sqrt(cells / region_count)
    return (back_v, back_h, total * scale)


def solution(mesh):
    in_specs = (
        P(("twin", "gx"), "gy", "gz"),
        P(("twin", "gx"), "gy", "gz"),
        P(("twin", "gx"), "gy", "gz"),
        P(("twin", "gx"), "gy", "gz"),
        P(("twin", "gx"), "gy", "gz"),
        P(("twin", "gx"), "gy", "gz"),
        P(("twin", "gx"), "gy", "gz"),
        P(("twin", "gx"), "gy", "gz"),
        P("twin", None),
        P("twin"),
    )
    out_specs = (P(("twin", "gx"), "gy", "gz"), P(("twin", "gx"), "gy", "gz"), P("twin"))
    return jax.shard_map(local, mesh=mesh, in_specs=in_specs, out_specs=out_specs, check_vma=False)
```

profile of v0, /device:TPU:0, one launch (start us, length us, event | category | flops | bytes accessed | tf_op | source)
XLA Modules:
  0.0 217.4 jit_solution(543356595917093015)
XLA Ops:
  1.4 4.9 %collective-permute-start.7 = (f32[1,16,128]{2,1,0:T(8,128)S(1)}, f32[1,16,128]{2,1,0:T(8,128)S(1)}, u32[]{:S(2)}, u32[]{:S(2)}) collective-permute-start(f32[1,16,128]{2,1,0:T(8,128)S(1)} %get-tuple-element.115), channel_id=1, source_target_pairs={{0,4},{4,8},{8,12},{1,5},{5,9},{9,13},{2,6},{6,10},{10,14},{3,7},{... | collective-permute-start | bytes 24584 | tf_op jit(solution)/shard_map/ppermute | solution.py:36
  11.6 11.1 %add_multiply_fusion.3 = f32[8,16,128]{2,1,0:T(8,128)S(1)} fusion(s32[8,16,128]{2,1,0:T(8,128)} %param.15, s32[8,16,128]{2,1,0:T(8,128)} %param.17, f32[]{:T(128)} %bitcast.15, f32[]{:T(128)} %bitcast.14, f32[]{:T(128)} %bitcast.13, f32[]{:T(128)} %bitcast.12, f32[]{:T(128)} %bitcast.11, f32[]{:T(128)} %bitcast.10, f32[]{:T(128)} %bitcast.9, f32[]{:T(128)} %bitcast.8, ...), kind=kLoop, calls=%fused_computation.360 | loop fusion | flops 802816 | bytes 196672 | tf_op jit(solution)/shard_map/mul | solution.py:126
  26.6 4.4 %collective-permute-start = (f32[9,1,16,128]{3,2,1,0:T(8,128)S(1)}, f32[9,1,16,128]{3,2,1,0:T(8,128)S(1)}, u32[]{:S(2)}, u32[]{:S(2)}) collective-permute-start(f32[9,1,16,128]{3,2,1,0:T(8,128)S(1)} %get-tuple-element.45), channel_id=1, source_target_pairs={{0,4},{4,8},{8,12},{1,5},{5,9},{9,13},{2,6},{6,10},{10,14},{3,7},{... | collective-permute-start | bytes 221192 | tf_op jit(solution)/shard_map/ppermute | solution.py:36
  33.5 4.4 %collective-permute-done.1 = f32[9,1,16,128]{3,2,1,0:T(8,128)S(1)} collective-permute-done((f32[9,1,16,128]{3,2,1,0:T(8,128)S(1)}, f32[9,1,16,128]{3,2,1,0:T(8,128)S(1)}, u32[]{:S(2)}, u32[]{:S(2)}) %collective-permute-start.1) | collective-permute-done | bytes 73760 | tf_op jit(solution)/shard_map/ppermute | solution.py:37
  41.2 3.4 %collective-permute-start.11 = (f32[10,18,1]{2,1,0:T(8,128)S(1)}, f32[10,18,1]{2,1,0:T(8,128)S(1)}, u32[]{:S(2)}, u32[]{:S(2)}) collective-permute-start(f32[10,18,1]{2,1,0:T(8,128)S(1)} %get-tuple-element.57), channel_id=1, source_target_pairs={{0,1},{2,3},{4,5},{6,7},{8,9},{10,11},{12,13},{14,15},{16,17},{18,... | collective-permute-start | bytes 2168 | tf_op jit(solution)/shard_map/ppermute | solution.py:36
  47.5 2.5 %copy.166 = f32[9,10,18,1]{2,3,1,0:T(1,128)} copy(f32[9,10,18,1]{3,2,1,0:T(8,128)} %get-tuple-element.41) | data formatting | bytes 12960
  51.9 5.8 %collective-permute-start.4 = (f32[9,10,18,1]{2,3,1,0:T(1,128)}, f32[9,10,18,1]{2,3,1,0:T(1,128)}, u32[]{:S(2)}, u32[]{:S(2)}) collective-permute-start(f32[9,10,18,1]{2,3,1,0:T(1,128)} %copy.166), channel_id=1, source_target_pairs={{0,1},{2,3},{4,5},{6,7},{8,9},{10,11},{12,13},{14,15},{16,17},{18,... | collective-permute-start | bytes 19448 | tf_op jit(solution)/shard_map/ppermute | solution.py:36
  60.6 2.4 %copy.158 = f32[9,10,18,1]{3,2,1,0:T(8,128)} copy(f32[9,10,18,1]{2,3,1,0:T(1,128)} %collective-permute-done.5) | data formatting | bytes 12960 | tf_op jit(solution)/shard_map/ppermute | solution.py:37
  63.0 2.6 %pad_maximum_fusion = f32[9,10,18,130]{3,2,1,0:T(8,128)S(1)} fusion(f32[9,10,18,1]{3,2,1,0:T(8,128)} %copy.158, f32[9,10,1,128]{3,2,1,0:T(1,128)S(1)} %collective-permute-done.3, f32[9,1,16,128]{3,2,1,0:T(8,128)S(1)} %collective-permute-done.1, f32[9,8,16,128]{3,2,1,0:T(8,128)S(1)} %get-tuple-element.30, f32[9,1,16,128]{3,2,1,0:T(8,128)S(1)} %collective-permute-done, ...), kind=kLoop, calls=%fused_computation | loop fusion | flops 1263600 | bytes 1684800 | tf_op jit(solution)/shard_map/concatenate | solution.py:38
  67.4 3.5 %collective-permute-start.13 = (f32[1,16,128]{2,1,0:T(8,128)S(1)}, f32[1,16,128]{2,1,0:T(8,128)S(1)}, u32[]{:S(2)}, u32[]{:S(2)}) collective-permute-start(f32[1,16,128]{2,1,0:T(8,128)S(1)} %get-tuple-element.101), channel_id=1, source_target_pairs={{0,4},{4,8},{8,12},{1,5},{5,9},{9,13},{2,6},{6,10},{10,14},{3,7},{... | collective-permute-start | bytes 24584 | tf_op jit(solution)/shard_map/ppermute | solution.py:36
  72.3 4.2 %collective-permute-done.12 = f32[1,16,128]{2,1,0:T(8,128)S(1)} collective-permute-done((f32[1,16,128]{2,1,0:T(8,128)S(1)}, f32[1,16,128]{2,1,0:T(8,128)S(1)}, u32[]{:S(2)}, u32[]{:S(2)}) %collective-permute-start.12) | collective-permute-done | bytes 8224 | tf_op jit(solution)/shard_map/ppermute | solution.py:37
  81.0 4.3 %collective-permute-start.17 = (f32[10,18,1]{2,1,0:T(8,128)S(1)}, f32[10,18,1]{2,1,0:T(8,128)S(1)}, u32[]{:S(2)}, u32[]{:S(2)}) collective-permute-start(f32[10,18,1]{2,1,0:T(8,128)S(1)} %get-tuple-element.55), channel_id=1, source_target_pairs={{0,1},{2,3},{4,5},{6,7},{8,9},{10,11},{12,13},{14,15},{16,17},{18,... | collective-permute-start | bytes 2168 | tf_op jit(solution)/shard_map/ppermute | solution.py:36
  88.2 4.1 %collective-permute-done.16 = f32[10,18,1]{2,1,0:T(8,128)S(1)} collective-permute-done((f32[10,18,1]{2,1,0:T(8,128)S(1)}, f32[10,18,1]{2,1,0:T(8,128)S(1)}, u32[]{:S(2)}, u32[]{:S(2)}) %collective-permute-start.16) | collective-permute-done | bytes 752 | tf_op jit(solution)/shard_map/ppermute | solution.py:37
  92.8 3.6 %collective-permute-start.19 = (f32[1,16,128]{2,1,0:T(8,128)S(1)}, f32[1,16,128]{2,1,0:T(8,128)S(1)}, u32[]{:S(2)}, u32[]{:S(2)}) collective-permute-start(f32[1,16,128]{2,1,0:T(8,128)S(1)} %get-tuple-element.99), channel_id=1, source_target_pairs={{0,4},{4,8},{8,12},{1,5},{5,9},{9,13},{2,6},{6,10},{10,14},{3,7},{... | collective-permute-start | bytes 24584 | tf_op jit(solution)/shard_map/ppermute | solution.py:36
  97.8 4.2 %collective-permute-done.18 = f32[1,16,128]{2,1,0:T(8,128)S(1)} collective-permute-done((f32[1,16,128]{2,1,0:T(8,128)S(1)}, f32[1,16,128]{2,1,0:T(8,128)S(1)}, u32[]{:S(2)}, u32[]{:S(2)}) %collective-permute-start.18) | collective-permute-done | bytes 8224 | tf_op jit(solution)/shard_map/ppermute | solution.py:37
  111.0 4.1 %collective-permute-done.22 = f32[10,18,1]{2,1,0:T(8,128)S(1)} collective-permute-done((f32[10,18,1]{2,1,0:T(8,128)S(1)}, f32[10,18,1]{2,1,0:T(8,128)S(1)}, u32[]{:S(2)}, u32[]{:S(2)}) %collective-permute-start.22) | collective-permute-done | bytes 752 | tf_op jit(solution)/shard_map/ppermute | solution.py:37
  119.2 4.2 %collective-permute-done.24 = f32[1,16,128]{2,1,0:T(8,128)S(1)} collective-permute-done((f32[1,16,128]{2,1,0:T(8,128)S(1)}, f32[1,16,128]{2,1,0:T(8,128)S(1)}, u32[]{:S(2)}, u32[]{:S(2)}) %collective-permute-start.24) | collective-permute-done | bytes 8224 | tf_op jit(solution)/shard_map/ppermute | solution.py:37
  132.5 4.1 %collective-permute-done.28 = f32[10,18,1]{2,1,0:T(8,128)S(1)} collective-permute-done((f32[10,18,1]{2,1,0:T(8,128)S(1)}, f32[10,18,1]{2,1,0:T(8,128)S(1)}, u32[]{:S(2)}, u32[]{:S(2)}) %collective-permute-start.28) | collective-permute-done | bytes 752 | tf_op jit(solution)/shard_map/ppermute | solution.py:37
  141.4 3.5 %collective-permute-done.30 = f32[1,16,128]{2,1,0:T(8,128)S(1)} collective-permute-done((f32[1,16,128]{2,1,0:T(8,128)S(1)}, f32[1,16,128]{2,1,0:T(8,128)S(1)}, u32[]{:S(2)}, u32[]{:S(2)}) %collective-permute-start.30) | collective-permute-done | bytes 8224 | tf_op jit(solution)/shard_map/ppermute | solution.py:37
  154.0 4.1 %collective-permute-done.34 = f32[10,18,1]{2,1,0:T(8,128)S(1)} collective-permute-done((f32[10,18,1]{2,1,0:T(8,128)S(1)}, f32[10,18,1]{2,1,0:T(8,128)S(1)}, u32[]{:S(2)}, u32[]{:S(2)}) %collective-permute-start.34) | collective-permute-done | bytes 752 | tf_op jit(solution)/shard_map/ppermute | solution.py:37
  163.1 3.6 %collective-permute-done.36 = f32[1,16,128]{2,1,0:T(8,128)S(1)} collective-permute-done((f32[1,16,128]{2,1,0:T(8,128)S(1)}, f32[1,16,128]{2,1,0:T(8,128)S(1)}, u32[]{:S(2)}, u32[]{:S(2)}) %collective-permute-start.36) | collective-permute-done | bytes 8224 | tf_op jit(solution)/shard_map/ppermute | solution.py:37
  176.0 4.1 %collective-permute-done.40 = f32[10,18,1]{2,1,0:T(8,128)S(1)} collective-permute-done((f32[10,18,1]{2,1,0:T(8,128)S(1)}, f32[10,18,1]{2,1,0:T(8,128)S(1)}, u32[]{:S(2)}, u32[]{:S(2)}) %collective-permute-start.40) | collective-permute-done | bytes 752 | tf_op jit(solution)/shard_map/ppermute | solution.py:37
  183.9 29.5 %psum.25 = f32[16]{0:T(128)S(1)} all-reduce(f32[16]{0:T(128)S(1)} %fusion), channel_id=1, replica_groups=mesh['twin'=2,'gx'=4,'gy'=2,'gz'=2] {'gx','gy','gz'}, use_global_device_ids=true, to_apply=%region_0.1 | all-reduce | flops 16 | bytes 128 | tf_op jit(solution)/shard_map/psum | solution.py:174
  214.0 3.4 %fusion.14 = f32[8,16,128]{2,1,0:T(8,128)} fusion(f32[8,16,128]{2,1,0:T(8,128)} %param.11, f32[8,16,128]{2,1,0:T(8,128)S(1)} %copy-done.30, f32[8,16,128]{2,1,0:T(8,128)} %copy-done.16, f32[8,16,128]{2,1,0:T(8,128)} %copy-done.15, f32[8,16,128]{2,1,0:T(8,128)} %copy-done.14, f32[8,16,128]{2,1,0:T(8,128)} %copy-done.13, f32[8,16,128]{2,1,0:T(8,128)} %copy-done.12, ...), kind=kLoop, calls=%fused_computation.82 | loop fusion | flops 5701632 | bytes 6291456 | tf_op jit(solution)/shard_map/add | solution.py:180
  (242 shorter events, 89.1 us)
Async XLA Ops:
  1.4 22.3 %collective-permute-start.7 = (f32[1,16,128]{2,1,0:T(8,128)S(1)}, f32[1,16,128]{2,1,0:T(8,128)S(1)}, u32[]{:S(2)}, u32[]{:S(2)}) collective-permute-start(f32[1,16,128]{2,1,0:T(8,128)S(1)} %get-tuple-element.115), channel_id=1, source_target_pairs={{0,4},{4,8},{8,12},{1,5},{5,9},{9,13},{2,6},{6,10},{10,14},{3,7},{... | collective-permute-start | bytes 24584 | tf_op jit(solution)/shard_map/ppermute | solution.py:36
  6.4 17.4 %collective-permute-start.6 = (f32[1,16,128]{2,1,0:T(8,128)S(1)}, f32[1,16,128]{2,1,0:T(8,128)S(1)}, u32[]{:S(2)}, u32[]{:S(2)}) collective-permute-start(f32[1,16,128]{2,1,0:T(8,128)S(1)} %get-tuple-element.116), channel_id=1, source_target_pairs={{4,0},{8,4},{12,8},{5,1},{9,5},{13,9},{6,2},{10,6},{14,10},{7,3},{... | collective-permute-start | bytes 24584 | tf_op jit(solution)/shard_map/ppermute | solution.py:37
  23.8 8.5 %collective-permute-start.9 = (f32[10,1,128]{2,1,0:T(1,128)S(1)}, f32[10,1,128]{2,1,0:T(1,128)S(1)}, u32[]{:S(2)}, u32[]{:S(2)}) collective-permute-start(f32[10,1,128]{2,1,0:T(1,128)S(1)} %get-tuple-element.91), channel_id=1, source_target_pairs={{0,2},{1,3},{4,6},{5,7},{8,10},{9,11},{12,14},{13,15},{16,18},{17,... | collective-permute-start | bytes 15368 | tf_op jit(solution)/shard_map/ppermute | solution.py:36
  25.3 7.0 %collective-permute-start.8 = (f32[10,1,128]{2,1,0:T(1,128)S(1)}, f32[10,1,128]{2,1,0:T(1,128)S(1)}, u32[]{:S(2)}, u32[]{:S(2)}) collective-permute-start(f32[10,1,128]{2,1,0:T(1,128)S(1)} %get-tuple-element.92), channel_id=1, source_target_pairs={{2,0},{3,1},{6,4},{7,5},{10,8},{11,9},{14,12},{15,13},{18,16},{19,... | collective-permute-start | bytes 15368 | tf_op jit(solution)/shard_map/ppermute | solution.py:37
  26.6 6.9 %collective-permute-start = (f32[9,1,16,128]{3,2,1,0:T(8,128)S(1)}, f32[9,1,16,128]{3,2,1,0:T(8,128)S(1)}, u32[]{:S(2)}, u32[]{:S(2)}) collective-permute-start(f32[9,1,16,128]{3,2,1,0:T(8,128)S(1)} %get-tuple-element.45), channel_id=1, source_target_pairs={{0,4},{4,8},{8,12},{1,5},{5,9},{9,13},{2,6},{6,10},{10,14},{3,7},{... | collective-permute-start | bytes 221192 | tf_op jit(solution)/shard_map/ppermute | solution.py:36
  31.0 6.9 %collective-permute-start.1 = (f32[9,1,16,128]{3,2,1,0:T(8,128)S(1)}, f32[9,1,16,128]{3,2,1,0:T(8,128)S(1)}, u32[]{:S(2)}, u32[]{:S(2)}) collective-permute-start(f32[9,1,16,128]{3,2,1,0:T(8,128)S(1)} %get-tuple-element.46), channel_id=1, source_target_pairs={{4,0},{8,4},{12,8},{5,1},{9,5},{13,9},{6,2},{10,6},{14,10},{7,3},{... | collective-permute-start | bytes 221192 | tf_op jit(solution)/shard_map/ppermute | solution.py:37
  37.9 8.0 %collective-permute-start.2 = (f32[9,10,1,128]{3,2,1,0:T(1,128)S(1)}, f32[9,10,1,128]{3,2,1,0:T(1,128)S(1)}, u32[]{:S(2)}, u32[]{:S(2)}) collective-permute-start(f32[9,10,1,128]{3,2,1,0:T(1,128)S(1)} %get-tuple-element.43), channel_id=1, source_target_pairs={{0,2},{1,3},{4,6},{5,7},{8,10},{9,11},{12,14},{13,15},{16,18},{17,... | collective-permute-start | bytes 138248 | tf_op jit(solution)/shard_map/ppermute | solution.py:36
  39.8 6.1 %collective-permute-start.3 = (f32[9,10,1,128]{3,2,1,0:T(1,128)S(1)}, f32[9,10,1,128]{3,2,1,0:T(1,128)S(1)}, u32[]{:S(2)}, u32[]{:S(2)}) collective-permute-start(f32[9,10,1,128]{3,2,1,0:T(1,128)S(1)} %get-tuple-element.44), channel_id=1, source_target_pairs={{2,0},{3,1},{6,4},{7,5},{10,8},{11,9},{14,12},{15,13},{18,16},{19,... | collective-permute-start | bytes 138248 | tf_op jit(solution)/shard_map/ppermute | solution.py:37
  41.2 16.5 %collective-permute-start.11 = (f32[10,18,1]{2,1,0:T(8,128)S(1)}, f32[10,18,1]{2,1,0:T(8,128)S(1)}, u32[]{:S(2)}, u32[]{:S(2)}) collective-permute-start(f32[10,18,1]{2,1,0:T(8,128)S(1)} %get-tuple-element.57), channel_id=1, source_target_pairs={{0,1},{2,3},{4,5},{6,7},{8,9},{10,11},{12,13},{14,15},{16,17},{18,... | collective-permute-start | bytes 2168 | tf_op jit(solution)/shard_map/ppermute | solution.py:36
  44.6 13.1 %collective-permute-start.10 = (f32[10,18,1]{2,1,0:T(8,128)S(1)}, f32[10,18,1]{2,1,0:T(8,128)S(1)}, u32[]{:S(2)}, u32[]{:S(2)}) collective-permute-start(f32[10,18,1]{2,1,0:T(8,128)S(1)} %get-tuple-element.58), channel_id=1, source_target_pairs={{1,0},{3,2},{5,4},{7,6},{9,8},{11,10},{13,12},{15,14},{17,16},{19,... | collective-permute-start | bytes 2168 | tf_op jit(solution)/shard_map/ppermute | solution.py:37
  50.6 9.9 %collective-permute-start.5 = (f32[9,10,18,1]{2,3,1,0:T(1,128)S(1)}, f32[9,10,18,1]{2,3,1,0:T(1,128)}, u32[]{:S(2)}, u32[]{:S(2)}) collective-permute-start(f32[9,10,18,1]{2,3,1,0:T(1,128)S(1)} %copy.167), channel_id=1, source_target_pairs={{1,0},{3,2},{5,4},{7,6},{9,8},{11,10},{13,12},{15,14},{17,16},{19,... | collective-permute-start | bytes 19448 | tf_op jit(solution)/shard_map/ppermute | solution.py:37
  51.9 7.2 %collective-permute-start.4 = (f32[9,10,18,1]{2,3,1,0:T(1,128)}, f32[9,10,18,1]{2,3,1,0:T(1,128)}, u32[]{:S(2)}, u32[]{:S(2)}) collective-permute-start(f32[9,10,18,1]{2,3,1,0:T(1,128)} %copy.166), channel_id=1, source_target_pairs={{0,1},{2,3},{4,5},{6,7},{8,9},{10,11},{12,13},{14,15},{16,17},{18,... | collective-permute-start | bytes 19448 | tf_op jit(solution)/shard_map/ppermute | solution.py:36
  70.9 5.5 %collective-permute-start.12 = (f32[1,16,128]{2,1,0:T(8,128)S(1)}, f32[1,16,128]{2,1,0:T(8,128)S(1)}, u32[]{:S(2)}, u32[]{:S(2)}) collective-permute-start(f32[1,16,128]{2,1,0:T(8,128)S(1)} %get-tuple-element.102), channel_id=1, source_target_pairs={{4,0},{8,4},{12,8},{5,1},{9,5},{13,9},{6,2},{10,6},{14,10},{7,3},{... | collective-permute-start | bytes 24584 | tf_op jit(solution)/shard_map/ppermute | solution.py:37
  81.0 7.2 %collective-permute-start.17 = (f32[10,18,1]{2,1,0:T(8,128)S(1)}, f32[10,18,1]{2,1,0:T(8,128)S(1)}, u32[]{:S(2)}, u32[]{:S(2)}) collective-permute-start(f32[10,18,1]{2,1,0:T(8,128)S(1)} %get-tuple-element.55), channel_id=1, source_target_pairs={{0,1},{2,3},{4,5},{6,7},{8,9},{10,11},{12,13},{14,15},{16,17},{18,... | collective-permute-start | bytes 2168 | tf_op jit(solution)/shard_map/ppermute | solution.py:36
  85.3 7.0 %collective-permute-start.16 = (f32[10,18,1]{2,1,0:T(8,128)S(1)}, f32[10,18,1]{2,1,0:T(8,128)S(1)}, u32[]{:S(2)}, u32[]{:S(2)}) collective-permute-start(f32[10,18,1]{2,1,0:T(8,128)S(1)} %get-tuple-element.56), channel_id=1, source_target_pairs={{1,0},{3,2},{5,4},{7,6},{9,8},{11,10},{13,12},{15,14},{17,16},{19,... | collective-permute-start | bytes 2168 | tf_op jit(solution)/shard_map/ppermute | solution.py:37
  92.8 5.0 %collective-permute-start.19 = (f32[1,16,128]{2,1,0:T(8,128)S(1)}, f32[1,16,128]{2,1,0:T(8,128)S(1)}, u32[]{:S(2)}, u32[]{:S(2)}) collective-permute-start(f32[1,16,128]{2,1,0:T(8,128)S(1)} %get-tuple-element.99), channel_id=1, source_target_pairs={{0,4},{4,8},{8,12},{1,5},{5,9},{9,13},{2,6},{6,10},{10,14},{3,7},{... | collective-permute-start | bytes 24584 | tf_op jit(solution)/shard_map/ppermute | solution.py:36
  96.5 5.5 %collective-permute-start.18 = (f32[1,16,128]{2,1,0:T(8,128)S(1)}, f32[1,16,128]{2,1,0:T(8,128)S(1)}, u32[]{:S(2)}, u32[]{:S(2)}) collective-permute-start(f32[1,16,128]{2,1,0:T(8,128)S(1)} %get-tuple-element.100), channel_id=1, source_target_pairs={{4,0},{8,4},{12,8},{5,1},{9,5},{13,9},{6,2},{10,6},{14,10},{7,3},{... | collective-permute-start | bytes 24584 | tf_op jit(solution)/shard_map/ppermute | solution.py:37
  108.0 7.1 %collective-permute-start.22 = (f32[10,18,1]{2,1,0:T(8,128)S(1)}, f32[10,18,1]{2,1,0:T(8,128)S(1)}, u32[]{:S(2)}, u32[]{:S(2)}) collective-permute-start(f32[10,18,1]{2,1,0:T(8,128)S(1)} %get-tuple-element.54), channel_id=1, source_target_pairs={{1,0},{3,2},{5,4},{7,6},{9,8},{11,10},{13,12},{15,14},{17,16},{19,... | collective-permute-start | bytes 2168 | tf_op jit(solution)/shard_map/ppermute | solution.py:37
  117.8 5.5 %collective-permute-start.24 = (f32[1,16,128]{2,1,0:T(8,128)S(1)}, f32[1,16,128]{2,1,0:T(8,128)S(1)}, u32[]{:S(2)}, u32[]{:S(2)}) collective-permute-start(f32[1,16,128]{2,1,0:T(8,128)S(1)} %get-tuple-element.98), channel_id=1, source_target_pairs={{4,0},{8,4},{12,8},{5,1},{9,5},{13,9},{6,2},{10,6},{14,10},{7,3},{... | collective-permute-start | bytes 24584 | tf_op jit(solution)/shard_map/ppermute | solution.py:37
  129.4 7.1 %collective-permute-start.28 = (f32[10,18,1]{2,1,0:T(8,128)S(1)}, f32[10,18,1]{2,1,0:T(8,128)S(1)}, u32[]{:S(2)}, u32[]{:S(2)}) collective-permute-start(f32[10,18,1]{2,1,0:T(8,128)S(1)} %get-tuple-element.52), channel_id=1, source_target_pairs={{1,0},{3,2},{5,4},{7,6},{9,8},{11,10},{13,12},{15,14},{17,16},{19,... | collective-permute-start | bytes 2168 | tf_op jit(solution)/shard_map/ppermute | solution.py:37
  139.3 5.5 %collective-permute-start.30 = (f32[1,16,128]{2,1,0:T(8,128)S(1)}, f32[1,16,128]{2,1,0:T(8,128)S(1)}, u32[]{:S(2)}, u32[]{:S(2)}) collective-permute-start(f32[1,16,128]{2,1,0:T(8,128)S(1)} %get-tuple-element.96), channel_id=1, source_target_pairs={{4,0},{8,4},{12,8},{5,1},{9,5},{13,9},{6,2},{10,6},{14,10},{7,3},{... | collective-permute-start | bytes 24584 | tf_op jit(solution)/shard_map/ppermute | solution.py:37
  150.8 7.3 %collective-permute-start.34 = (f32[10,18,1]{2,1,0:T(8,128)S(1)}, f32[10,18,1]{2,1,0:T(8,128)S(1)}, u32[]{:S(2)}, u32[]{:S(2)}) collective-permute-start(f32[10,18,1]{2,1,0:T(8,128)S(1)} %get-tuple-element.50), channel_id=1, source_target_pairs={{1,0},{3,2},{5,4},{7,6},{9,8},{11,10},{13,12},{15,14},{17,16},{19,... | collective-permute-start | bytes 2168 | tf_op jit(solution)/shard_map/ppermute | solution.py:37
  161.2 5.5 %collective-permute-start.36 = (f32[1,16,128]{2,1,0:T(8,128)S(1)}, f32[1,16,128]{2,1,0:T(8,128)S(1)}, u32[]{:S(2)}, u32[]{:S(2)}) collective-permute-start(f32[1,16,128]{2,1,0:T(8,128)S(1)} %get-tuple-element.94), channel_id=1, source_target_pairs={{4,0},{8,4},{12,8},{5,1},{9,5},{13,9},{6,2},{10,6},{14,10},{7,3},{... | collective-permute-start | bytes 24584 | tf_op jit(solution)/shard_map/ppermute | solution.py:37
  172.7 7.4 %collective-permute-start.40 = (f32[10,18,1]{2,1,0:T(8,128)S(1)}, f32[10,18,1]{2,1,0:T(8,128)S(1)}, u32[]{:S(2)}, u32[]{:S(2)}) collective-permute-start(f32[10,18,1]{2,1,0:T(8,128)S(1)} %get-tuple-element.48), channel_id=1, source_target_pairs={{1,0},{3,2},{5,4},{7,6},{9,8},{11,10},{13,12},{15,14},{17,16},{19,... | collective-permute-start | bytes 2168 | tf_op jit(solution)/shard_map/ppermute | solution.py:37
  (74 other events, 2827.3 us)
where the time goes:
time: 219 us; the launch traced here: 217 us
  starting transfers between devices  78.7 us (36%)
  waiting for transfers between devices  62.6 us (29%)
  blocking collectives  29.5 us (13%)
  other arithmetic  28.1 us (13%)
  local copies, waits for them, and re-layouts  13.7 us (6%)
  matrix products  2.53 us (1%)
  between operations  2.23 us (1%)
    ppermute x21, waiting for transfers between devices, extended(): after = lax.ppermute(initial, axis, down)  51.3 us
    ppermute x21, starting transfers between devices, extended(): before = lax.ppermute(last, axis, up)  51.3 us
    psum x1, blocking collectives, local(): total = total + lax.psum(partial_sums, ('gx', 'gy', 'gz'))  29.5 us
    ppermute x21, starting transfers between devices, extended(): after = lax.ppermute(initial, axis, down)  27.4 us
    mul x2, other arithmetic, local_coefficients(): flux_local = (tissue_local * local_factor)[None] * fibre_local  12.1 us
    ppermute x21, waiting for transfers between devices, extended(): before = lax.ppermute(last, axis, up)  11.3 us
  transfers between devices with their start and end apart: 42, of which 23 were waited for; matrix products, arithmetic and copies ran while one was open for 12% of the time, Pallas kernels for 0%

commit v1 on v0

--- a/solution.py
+++ b/solution.py
@@ -24,6 +24,12 @@
     (0, 1, 1),
     (0, 1, -1),
 )
+
+
+def add_all(x, axis):
+    parts = lax.all_gather(x, axis, axis=0, tiled=False)
+    total = parts.sum(axis=0)
+    return total
 
 
 def extended(array, sides, width):
@@ -171,7 +177,7 @@
         partial_sums = jnp.einsum(
             "rxyz,xyz->r", selector, terms, precision=jax.lax.Precision.HIGHEST
         )
-        total = total + lax.psum(partial_sums, ("gx", "gy", "gz"))
+        total = total + add_all(partial_sums, ("gx", "gy", "gz"))
         deriv_vv, deriv_vh, deriv_hv, deriv_hh = ionic_partials(
             crop(volts_pad, 1), saved_gates[step]
         )

time: 219 us -> 230 us (1.050)
  waiting for transfers between devices: 62.6 us -> 26.8 us
  starting transfers between devices: 78.7 us -> 109 us
  other arithmetic: 28.1 us -> 37.1 us
  blocking collectives: 29.5 us -> 32.9 us
    ppermute x21, waiting for transfers between devices: 51.3 us -> 13.8 us  [extended(): after = lax.ppermute(initial, axis, down)]
    unnamed x0 -> x1, blocking collectives: none -> 32.9 us
    ppermute x21, starting transfers between devices: 51.3 us -> 81.2 us  [extended(): before = lax.ppermute(last, axis, up)]
    psum x1 -> x0, blocking collectives: 29.5 us -> none  [local(): total = total + lax.psum(partial_sums, ('gx', 'gy', 'gz'))]
    mul x3, other arithmetic: 2.05 us -> 5.63 us  [local(): masked = tissue_local * back_v]
    concatenate x24, other arithmetic: 4.09 us -> 7.27 us  [extended(): array = jnp.concatenate([before, array, after], axis=dim)]
    unnamed x116 -> x273, local copies, waits for them, and re-layouts: 4 us -> 6.55 us
  transfers between devices with their start and end apart: 42 -> 42, of which waited for: 23 -> 19; matrix products, arithmetic and copies ran while one was open for 12% -> 13% of each run, Pallas kernels for 0% -> 0%
where the time goes in v1:
time: 230 us; the launch traced here: 228 us
  starting transfers between devices  109 us (47%)
  other arithmetic  37.1 us (16%)
  blocking collectives  32.9 us (14%)
  waiting for transfers between devices  26.8 us (12%)
  local copies, waits for them, and re-layouts  14.9 us (6%)
  between operations  4.08 us (2%)
  matrix products  3.34 us (1%)
    ppermute x21, starting transfers between devices, extended(): before = lax.ppermute(last, axis, up)  81.2 us
    unnamed x1, blocking collectives  32.9 us
    ppermute x21, starting transfers between devices, extended(): after = lax.ppermute(initial, axis, down)  27.7 us
    ppermute x21, waiting for transfers between devices, extended(): after = lax.ppermute(initial, axis, down)  13.8 us
    ppermute x21, waiting for transfers between devices, extended(): before = lax.ppermute(last, axis, up)  13.1 us
    mul x2, other arithmetic, local_coefficients(): flux_local = (tissue_local * local_factor)[None] * fibre_local  12.1 us
    concatenate x24, other arithmetic, extended(): array = jnp.concatenate([before, array, after], axis=dim)  7.27 us
    unnamed x273, local copies, waits for them, and re-layouts  6.55 us
  transfers between devices with their start and end apart: 42, of which 19 were waited for; matrix products, arithmetic and copies ran while one was open for 13% of the time, Pallas kernels for 0%

profile of v1, /device:TPU:0, one launch (start us, length us, event | category | flops | bytes accessed | tf_op | source)
XLA Modules:
  0.0 228.1 jit_solution(17368695246881135488)
XLA Ops:
  1.4 4.9 %collective-permute-start.7 = (f32[1,16,128]{2,1,0:T(8,128)S(1)}, f32[1,16,128]{2,1,0:T(8,128)S(1)}, u32[]{:S(2)}, u32[]{:S(2)}) collective-permute-start(f32[1,16,128]{2,1,0:T(8,128)S(1)} %get-tuple-element.118), channel_id=1, source_target_pairs={{0,4},{4,8},{8,12},{1,5},{5,9},{9,13},{2,6},{6,10},{10,14},{3,7},{... | collective-permute-start | bytes 24584 | tf_op jit(solution)/shard_map/ppermute | solution.py:42
  11.6 11.0 %add_multiply_fusion.3 = f32[8,16,128]{2,1,0:T(8,128)S(1)} fusion(s32[8,16,128]{2,1,0:T(8,128)} %param.15, s32[8,16,128]{2,1,0:T(8,128)} %param.17, f32[]{:T(128)} %bitcast.15, f32[]{:T(128)} %bitcast.14, f32[]{:T(128)} %bitcast.13, f32[]{:T(128)} %bitcast.12, f32[]{:T(128)} %bitcast.11, f32[]{:T(128)} %bitcast.10, f32[]{:T(128)} %bitcast.9, f32[]{:T(128)} %bitcast.8, ...), kind=kLoop, calls=%fused_computation.358 | loop fusion | flops 802816 | bytes 196672 | tf_op jit(solution)/shard_map/mul | solution.py:132
  25.1 3.0 %collective-permute-start.9 = (f32[10,1,128]{2,1,0:T(1,128)S(1)}, f32[10,1,128]{2,1,0:T(1,128)S(1)}, u32[]{:S(2)}, u32[]{:S(2)}) collective-permute-start(f32[10,1,128]{2,1,0:T(1,128)S(1)} %get-tuple-element.94), channel_id=1, source_target_pairs={{0,2},{1,3},{4,6},{5,7},{8,10},{9,11},{12,14},{13,15},{16,18},{17,... | collective-permute-start | bytes 15368 | tf_op jit(solution)/shard_map/ppermute | solution.py:42
  28.1 4.5 %collective-permute-start = (f32[9,1,16,128]{3,2,1,0:T(8,128)S(1)}, f32[9,1,16,128]{3,2,1,0:T(8,128)S(1)}, u32[]{:S(2)}, u32[]{:S(2)}) collective-permute-start(f32[9,1,16,128]{3,2,1,0:T(8,128)S(1)} %get-tuple-element.48), channel_id=1, source_target_pairs={{0,4},{4,8},{8,12},{1,5},{5,9},{9,13},{2,6},{6,10},{10,14},{3,7},{... | collective-permute-start | bytes 221192 | tf_op jit(solution)/shard_map/ppermute | solution.py:42
  34.7 4.3 %collective-permute-done.1 = f32[9,1,16,128]{3,2,1,0:T(8,128)S(1)} collective-permute-done((f32[9,1,16,128]{3,2,1,0:T(8,128)S(1)}, f32[9,1,16,128]{3,2,1,0:T(8,128)S(1)}, u32[]{:S(2)}, u32[]{:S(2)}) %collective-permute-start.1) | collective-permute-done | bytes 73760 | tf_op jit(solution)/shard_map/ppermute | solution.py:43
  43.0 4.6 %collective-permute-start.11 = (f32[10,18,1]{2,1,0:T(8,128)S(1)}, f32[10,18,1]{2,1,0:T(8,128)S(1)}, u32[]{:S(2)}, u32[]{:S(2)}) collective-permute-start(f32[10,18,1]{2,1,0:T(8,128)S(1)} %get-tuple-element.60), channel_id=1, source_target_pairs={{0,1},{2,3},{4,5},{6,7},{8,9},{10,11},{12,13},{14,15},{16,17},{18,... | collective-permute-start | bytes 2168 | tf_op jit(solution)/shard_map/ppermute | solution.py:42
  55.8 3.1 %collective-permute-done.5 = f32[9,10,18,1]{2,3,1,0:T(1,128)S(1)} collective-permute-done((f32[9,10,18,1]{2,3,1,0:T(1,128)S(1)}, f32[9,10,18,1]{2,3,1,0:T(1,128)S(1)}, u32[]{:S(2)}, u32[]{:S(2)}) %collective-permute-start.5) | collective-permute-done | bytes 6512 | tf_op jit(solution)/shard_map/ppermute | solution.py:43
  66.7 4.5 %collective-permute-start.13 = (f32[1,16,128]{2,1,0:T(8,128)S(1)}, f32[1,16,128]{2,1,0:T(8,128)S(1)}, u32[]{:S(2)}, u32[]{:S(2)}) collective-permute-start(f32[1,16,128]{2,1,0:T(8,128)S(1)} %get-tuple-element.104), channel_id=1, source_target_pairs={{0,4},{4,8},{8,12},{1,5},{5,9},{9,13},{2,6},{6,10},{10,14},{3,7},{... | collective-permute-start | bytes 24584 | tf_op jit(solution)/shard_map/ppermute | solution.py:42
  73.9 3.0 %collective-permute-start.15 = (f32[10,1,128]{2,1,0:T(1,128)S(1)}, f32[10,1,128]{2,1,0:T(1,128)S(1)}, u32[]{:S(2)}, u32[]{:S(2)}) collective-permute-start(f32[10,1,128]{2,1,0:T(1,128)S(1)} %get-tuple-element.92), channel_id=1, source_target_pairs={{0,2},{1,3},{4,6},{5,7},{8,10},{9,11},{12,14},{13,15},{16,18},{17,... | collective-permute-start | bytes 15368 | tf_op jit(solution)/shard_map/ppermute | solution.py:42
  79.2 4.6 %collective-permute-start.17 = (f32[10,18,1]{2,1,0:T(8,128)S(1)}, f32[10,18,1]{2,1,0:T(8,128)S(1)}, u32[]{:S(2)}, u32[]{:S(2)}) collective-permute-start(f32[10,18,1]{2,1,0:T(8,128)S(1)} %get-tuple-element.58), channel_id=1, source_target_pairs={{0,1},{2,3},{4,5},{6,7},{8,9},{10,11},{12,13},{14,15},{16,17},{18,... | collective-permute-start | bytes 2168 | tf_op jit(solution)/shard_map/ppermute | solution.py:42
  88.4 4.8 %collective-permute-start.19 = (f32[1,16,128]{2,1,0:T(8,128)S(1)}, f32[1,16,128]{2,1,0:T(8,128)S(1)}, u32[]{:S(2)}, u32[]{:S(2)}) collective-permute-start(f32[1,16,128]{2,1,0:T(8,128)S(1)} %get-tuple-element.102), channel_id=1, source_target_pairs={{0,4},{4,8},{8,12},{1,5},{5,9},{9,13},{2,6},{6,10},{10,14},{3,7},{... | collective-permute-start | bytes 24584 | tf_op jit(solution)/shard_map/ppermute | solution.py:42
  95.9 3.0 %collective-permute-start.21 = (f32[10,1,128]{2,1,0:T(1,128)S(1)}, f32[10,1,128]{2,1,0:T(1,128)S(1)}, u32[]{:S(2)}, u32[]{:S(2)}) collective-permute-start(f32[10,1,128]{2,1,0:T(1,128)S(1)} %get-tuple-element.88), channel_id=1, source_target_pairs={{0,2},{1,3},{4,6},{5,7},{8,10},{9,11},{12,14},{13,15},{16,18},{17,... | collective-permute-start | bytes 15368 | tf_op jit(solution)/shard_map/ppermute | solution.py:42
  101.2 4.6 %collective-permute-start.23 = (f32[10,18,1]{2,1,0:T(8,128)S(1)}, f32[10,18,1]{2,1,0:T(8,128)S(1)}, u32[]{:S(2)}, u32[]{:S(2)}) collective-permute-start(f32[10,18,1]{2,1,0:T(8,128)S(1)} %get-tuple-element.56), channel_id=1, source_target_pairs={{0,1},{2,3},{4,5},{6,7},{8,9},{10,11},{12,13},{14,15},{16,17},{18,... | collective-permute-start | bytes 2168 | tf_op jit(solution)/shard_map/ppermute | solution.py:42
  111.5 4.8 %collective-permute-start.25 = (f32[1,16,128]{2,1,0:T(8,128)S(1)}, f32[1,16,128]{2,1,0:T(8,128)S(1)}, u32[]{:S(2)}, u32[]{:S(2)}) collective-permute-start(f32[1,16,128]{2,1,0:T(8,128)S(1)} %get-tuple-element.100), channel_id=1, source_target_pairs={{0,4},{4,8},{8,12},{1,5},{5,9},{9,13},{2,6},{6,10},{10,14},{3,7},{... | collective-permute-start | bytes 24584 | tf_op jit(solution)/shard_map/ppermute | solution.py:42
  119.0 3.0 %collective-permute-start.27 = (f32[10,1,128]{2,1,0:T(1,128)S(1)}, f32[10,1,128]{2,1,0:T(1,128)S(1)}, u32[]{:S(2)}, u32[]{:S(2)}) collective-permute-start(f32[10,1,128]{2,1,0:T(1,128)S(1)} %get-tuple-element.84), channel_id=1, source_target_pairs={{0,2},{1,3},{4,6},{5,7},{8,10},{9,11},{12,14},{13,15},{16,18},{17,... | collective-permute-start | bytes 15368 | tf_op jit(solution)/shard_map/ppermute | solution.py:42
  125.6 4.6 %collective-permute-start.29 = (f32[10,18,1]{2,1,0:T(8,128)S(1)}, f32[10,18,1]{2,1,0:T(8,128)S(1)}, u32[]{:S(2)}, u32[]{:S(2)}) collective-permute-start(f32[10,18,1]{2,1,0:T(8,128)S(1)} %get-tuple-element.54), channel_id=1, source_target_pairs={{0,1},{2,3},{4,5},{6,7},{8,9},{10,11},{12,13},{14,15},{16,17},{18,... | collective-permute-start | bytes 2168 | tf_op jit(solution)/shard_map/ppermute | solution.py:42
  136.2 4.8 %collective-permute-start.31 = (f32[1,16,128]{2,1,0:T(8,128)S(1)}, f32[1,16,128]{2,1,0:T(8,128)S(1)}, u32[]{:S(2)}, u32[]{:S(2)}) collective-permute-start(f32[1,16,128]{2,1,0:T(8,128)S(1)} %get-tuple-element.98), channel_id=1, source_target_pairs={{0,4},{4,8},{8,12},{1,5},{5,9},{9,13},{2,6},{6,10},{10,14},{3,7},{... | collective-permute-start | bytes 24584 | tf_op jit(solution)/shard_map/ppermute | solution.py:42
  144.8 3.0 %collective-permute-start.33 = (f32[10,1,128]{2,1,0:T(1,128)S(1)}, f32[10,1,128]{2,1,0:T(1,128)S(1)}, u32[]{:S(2)}, u32[]{:S(2)}) collective-permute-start(f32[10,1,128]{2,1,0:T(1,128)S(1)} %get-tuple-element.80), channel_id=1, source_target_pairs={{0,2},{1,3},{4,6},{5,7},{8,10},{9,11},{12,14},{13,15},{16,18},{17,... | collective-permute-start | bytes 15368 | tf_op jit(solution)/shard_map/ppermute | solution.py:42
  151.0 4.6 %collective-permute-start.35 = (f32[10,18,1]{2,1,0:T(8,128)S(1)}, f32[10,18,1]{2,1,0:T(8,128)S(1)}, u32[]{:S(2)}, u32[]{:S(2)}) collective-permute-start(f32[10,18,1]{2,1,0:T(8,128)S(1)} %get-tuple-element.52), channel_id=1, source_target_pairs={{0,1},{2,3},{4,5},{6,7},{8,9},{10,11},{12,13},{14,15},{16,17},{18,... | collective-permute-start | bytes 2168 | tf_op jit(solution)/shard_map/ppermute | solution.py:42
  163.4 4.7 %collective-permute-start.37 = (f32[1,16,128]{2,1,0:T(8,128)S(1)}, f32[1,16,128]{2,1,0:T(8,128)S(1)}, u32[]{:S(2)}, u32[]{:S(2)}) collective-permute-start(f32[1,16,128]{2,1,0:T(8,128)S(1)} %get-tuple-element.96), channel_id=1, source_target_pairs={{0,4},{4,8},{8,12},{1,5},{5,9},{9,13},{2,6},{6,10},{10,14},{3,7},{... | collective-permute-start | bytes 24584 | tf_op jit(solution)/shard_map/ppermute | solution.py:42
  172.8 3.0 %collective-permute-start.39 = (f32[10,1,128]{2,1,0:T(1,128)S(1)}, f32[10,1,128]{2,1,0:T(1,128)S(1)}, u32[]{:S(2)}, u32[]{:S(2)}) collective-permute-start(f32[10,1,128]{2,1,0:T(1,128)S(1)} %get-tuple-element.76), channel_id=1, source_target_pairs={{0,2},{1,3},{4,6},{5,7},{8,10},{9,11},{12,14},{13,15},{16,18},{17,... | collective-permute-start | bytes 15368 | tf_op jit(solution)/shard_map/ppermute | solution.py:42
  180.2 4.6 %collective-permute-start.41 = (f32[10,18,1]{2,1,0:T(8,128)S(1)}, f32[10,18,1]{2,1,0:T(8,128)S(1)}, u32[]{:S(2)}, u32[]{:S(2)}) collective-permute-start(f32[10,18,1]{2,1,0:T(8,128)S(1)} %get-tuple-element.50), channel_id=1, source_target_pairs={{0,1},{2,3},{4,5},{6,7},{8,9},{10,11},{12,13},{14,15},{16,17},{18,... | collective-permute-start | bytes 2168 | tf_op jit(solution)/shard_map/ppermute | solution.py:42
  190.6 32.9 %all-reduce.3 = (f32[256]{0:T(256)S(1)}, f32[256]{0:T(256)S(1)}, f32[256]{0:T(256)S(1)}) all-reduce(f32[256]{0:T(256)S(1)} %dynamic-update-slice.2, f32[256]{0:T(256)} %copy-done.128, f32[256]{0:T(256)} %copy-done.129), channel_id=4, replica_groups=mesh['twin'=2,'gx'=4,'gy'=2,'gz'=2] {'gx','gy','gz'}, use_global_device_ids=true, to_apply=%add.2 | all-reduce | flops 768 | bytes 6144
  224.4 3.5 %fusion.12 = f32[8,16,128]{2,1,0:T(8,128)} fusion(f32[8,16,128]{2,1,0:T(8,128)} %param.11, f32[8,16,128]{2,1,0:T(8,128)} %param.10, f32[8,16,128]{2,1,0:T(8,128)} %copy-done.48, f32[8,16,128]{2,1,0:T(8,128)} %copy-done.45, f32[8,16,128]{2,1,0:T(8,128)} %copy-done.42, f32[8,16,128]{2,1,0:T(8,128)} %copy-done.39, f32[8,16,128]{2,1,0:T(8,128)} %copy-done.36, ...), kind=kLoop, calls=%fused_computation.80 | loop fusion | flops 5701632 | bytes 6291456 | tf_op jit(solution)/shard_map/add | solution.py:186
  (405 shorter events, 90.5 us)
Async XLA Ops:
  1.4 22.3 %collective-permute-start.7 = (f32[1,16,128]{2,1,0:T(8,128)S(1)}, f32[1,16,128]{2,1,0:T(8,128)S(1)}, u32[]{:S(2)}, u32[]{:S(2)}) collective-permute-start(f32[1,16,128]{2,1,0:T(8,128)S(1)} %get-tuple-element.118), channel_id=1, source_target_pairs={{0,4},{4,8},{8,12},{1,5},{5,9},{9,13},{2,6},{6,10},{10,14},{3,7},{... | collective-permute-start | bytes 24584 | tf_op jit(solution)/shard_map/ppermute | solution.py:42
  6.4 17.4 %collective-permute-start.6 = (f32[1,16,128]{2,1,0:T(8,128)S(1)}, f32[1,16,128]{2,1,0:T(8,128)S(1)}, u32[]{:S(2)}, u32[]{:S(2)}) collective-permute-start(f32[1,16,128]{2,1,0:T(8,128)S(1)} %get-tuple-element.119), channel_id=1, source_target_pairs={{4,0},{8,4},{12,8},{5,1},{9,5},{13,9},{6,2},{10,6},{14,10},{7,3},{... | collective-permute-start | bytes 24584 | tf_op jit(solution)/shard_map/ppermute | solution.py:43
  23.8 10.2 %collective-permute-start.8 = (f32[10,1,128]{2,1,0:T(1,128)S(1)}, f32[10,1,128]{2,1,0:T(1,128)S(1)}, u32[]{:S(2)}, u32[]{:S(2)}) collective-permute-start(f32[10,1,128]{2,1,0:T(1,128)S(1)} %get-tuple-element.95), channel_id=1, source_target_pairs={{2,0},{3,1},{6,4},{7,5},{10,8},{11,9},{14,12},{15,13},{18,16},{19,... | collective-permute-start | bytes 15368 | tf_op jit(solution)/shard_map/ppermute | solution.py:43
  25.1 9.0 %collective-permute-start.9 = (f32[10,1,128]{2,1,0:T(1,128)S(1)}, f32[10,1,128]{2,1,0:T(1,128)S(1)}, u32[]{:S(2)}, u32[]{:S(2)}) collective-permute-start(f32[10,1,128]{2,1,0:T(1,128)S(1)} %get-tuple-element.94), channel_id=1, source_target_pairs={{0,2},{1,3},{4,6},{5,7},{8,10},{9,11},{12,14},{13,15},{16,18},{17,... | collective-permute-start | bytes 15368 | tf_op jit(solution)/shard_map/ppermute | solution.py:42
  28.1 6.5 %collective-permute-start = (f32[9,1,16,128]{3,2,1,0:T(8,128)S(1)}, f32[9,1,16,128]{3,2,1,0:T(8,128)S(1)}, u32[]{:S(2)}, u32[]{:S(2)}) collective-permute-start(f32[9,1,16,128]{3,2,1,0:T(8,128)S(1)} %get-tuple-element.48), channel_id=1, source_target_pairs={{0,4},{4,8},{8,12},{1,5},{5,9},{9,13},{2,6},{6,10},{10,14},{3,7},{... | collective-permute-start | bytes 221192 | tf_op jit(solution)/shard_map/ppermute | solution.py:42
  39.0 8.6 %collective-permute-start.2 = (f32[9,10,1,128]{3,2,1,0:T(1,128)S(1)}, f32[9,10,1,128]{3,2,1,0:T(1,128)S(1)}, u32[]{:S(2)}, u32[]{:S(2)}) collective-permute-start(f32[9,10,1,128]{3,2,1,0:T(1,128)S(1)} %get-tuple-element.46), channel_id=1, source_target_pairs={{0,2},{1,3},{4,6},{5,7},{8,10},{9,11},{12,14},{13,15},{16,18},{17,... | collective-permute-start | bytes 138248 | tf_op jit(solution)/shard_map/ppermute | solution.py:42
  40.3 7.3 %collective-permute-start.3 = (f32[9,10,1,128]{3,2,1,0:T(1,128)S(1)}, f32[9,10,1,128]{3,2,1,0:T(1,128)S(1)}, u32[]{:S(2)}, u32[]{:S(2)}) collective-permute-start(f32[9,10,1,128]{3,2,1,0:T(1,128)S(1)} %get-tuple-element.47), channel_id=1, source_target_pairs={{2,0},{3,1},{6,4},{7,5},{10,8},{11,9},{14,12},{15,13},{18,16},{19,... | collective-permute-start | bytes 138248 | tf_op jit(solution)/shard_map/ppermute | solution.py:43
  41.7 12.5 %collective-permute-start.10 = (f32[10,18,1]{2,1,0:T(8,128)S(1)}, f32[10,18,1]{2,1,0:T(8,128)S(1)}, u32[]{:S(2)}, u32[]{:S(2)}) collective-permute-start(f32[10,18,1]{2,1,0:T(8,128)S(1)} %get-tuple-element.61), channel_id=1, source_target_pairs={{1,0},{3,2},{5,4},{7,6},{9,8},{11,10},{13,12},{15,14},{17,16},{19,... | collective-permute-start | bytes 2168 | tf_op jit(solution)/shard_map/ppermute | solution.py:43
  43.0 11.2 %collective-permute-start.11 = (f32[10,18,1]{2,1,0:T(8,128)S(1)}, f32[10,18,1]{2,1,0:T(8,128)S(1)}, u32[]{:S(2)}, u32[]{:S(2)}) collective-permute-start(f32[10,18,1]{2,1,0:T(8,128)S(1)} %get-tuple-element.60), channel_id=1, source_target_pairs={{0,1},{2,3},{4,5},{6,7},{8,9},{10,11},{12,13},{14,15},{16,17},{18,... | collective-permute-start | bytes 2168 | tf_op jit(solution)/shard_map/ppermute | solution.py:42
  77.9 7.5 %collective-permute-start.16 = (f32[10,18,1]{2,1,0:T(8,128)S(1)}, f32[10,18,1]{2,1,0:T(8,128)S(1)}, u32[]{:S(2)}, u32[]{:S(2)}) collective-permute-start(f32[10,18,1]{2,1,0:T(8,128)S(1)} %get-tuple-element.59), channel_id=1, source_target_pairs={{1,0},{3,2},{5,4},{7,6},{9,8},{11,10},{13,12},{15,14},{17,16},{19,... | collective-permute-start | bytes 2168 | tf_op jit(solution)/shard_map/ppermute | solution.py:43
  79.2 7.3 %collective-permute-start.17 = (f32[10,18,1]{2,1,0:T(8,128)S(1)}, f32[10,18,1]{2,1,0:T(8,128)S(1)}, u32[]{:S(2)}, u32[]{:S(2)}) collective-permute-start(f32[10,18,1]{2,1,0:T(8,128)S(1)} %get-tuple-element.58), channel_id=1, source_target_pairs={{0,1},{2,3},{4,5},{6,7},{8,9},{10,11},{12,13},{14,15},{16,17},{18,... | collective-permute-start | bytes 2168 | tf_op jit(solution)/shard_map/ppermute | solution.py:42
  99.9 7.6 %collective-permute-start.22 = (f32[10,18,1]{2,1,0:T(8,128)S(1)}, f32[10,18,1]{2,1,0:T(8,128)S(1)}, u32[]{:S(2)}, u32[]{:S(2)}) collective-permute-start(f32[10,18,1]{2,1,0:T(8,128)S(1)} %get-tuple-element.57), channel_id=1, source_target_pairs={{1,0},{3,2},{5,4},{7,6},{9,8},{11,10},{13,12},{15,14},{17,16},{19,... | collective-permute-start | bytes 2168 | tf_op jit(solution)/shard_map/ppermute | solution.py:43
  101.2 7.5 %collective-permute-start.23 = (f32[10,18,1]{2,1,0:T(8,128)S(1)}, f32[10,18,1]{2,1,0:T(8,128)S(1)}, u32[]{:S(2)}, u32[]{:S(2)}) collective-permute-start(f32[10,18,1]{2,1,0:T(8,128)S(1)} %get-tuple-element.56), channel_id=1, source_target_pairs={{0,1},{2,3},{4,5},{6,7},{8,9},{10,11},{12,13},{14,15},{16,17},{18,... | collective-permute-start | bytes 2168 | tf_op jit(solution)/shard_map/ppermute | solution.py:42
  117.7 6.4 %collective-permute-start.26 = (f32[10,1,128]{2,1,0:T(1,128)S(1)}, f32[10,1,128]{2,1,0:T(1,128)S(1)}, u32[]{:S(2)}, u32[]{:S(2)}) collective-permute-start(f32[10,1,128]{2,1,0:T(1,128)S(1)} %get-tuple-element.85), channel_id=1, source_target_pairs={{2,0},{3,1},{6,4},{7,5},{10,8},{11,9},{14,12},{15,13},{18,16},{19,... | collective-permute-start | bytes 15368 | tf_op jit(solution)/shard_map/ppermute | solution.py:43
  124.3 6.8 %collective-permute-start.28 = (f32[10,18,1]{2,1,0:T(8,128)S(1)}, f32[10,18,1]{2,1,0:T(8,128)S(1)}, u32[]{:S(2)}, u32[]{:S(2)}) collective-permute-start(f32[10,18,1]{2,1,0:T(8,128)S(1)} %get-tuple-element.55), channel_id=1, source_target_pairs={{1,0},{3,2},{5,4},{7,6},{9,8},{11,10},{13,12},{15,14},{17,16},{19,... | collective-permute-start | bytes 2168 | tf_op jit(solution)/shard_map/ppermute | solution.py:43
  125.6 7.0 %collective-permute-start.29 = (f32[10,18,1]{2,1,0:T(8,128)S(1)}, f32[10,18,1]{2,1,0:T(8,128)S(1)}, u32[]{:S(2)}, u32[]{:S(2)}) collective-permute-start(f32[10,18,1]{2,1,0:T(8,128)S(1)} %get-tuple-element.54), channel_id=1, source_target_pairs={{0,1},{2,3},{4,5},{6,7},{8,9},{10,11},{12,13},{14,15},{16,17},{18,... | collective-permute-start | bytes 2168 | tf_op jit(solution)/shard_map/ppermute | solution.py:42
  134.9 7.1 %collective-permute-start.30 = (f32[1,16,128]{2,1,0:T(8,128)S(1)}, f32[1,16,128]{2,1,0:T(8,128)S(1)}, u32[]{:S(2)}, u32[]{:S(2)}) collective-permute-start(f32[1,16,128]{2,1,0:T(8,128)S(1)} %get-tuple-element.99), channel_id=1, source_target_pairs={{4,0},{8,4},{12,8},{5,1},{9,5},{13,9},{6,2},{10,6},{14,10},{7,3},{... | collective-permute-start | bytes 24584 | tf_op jit(solution)/shard_map/ppermute | solution.py:43
  149.7 7.3 %collective-permute-start.34 = (f32[10,18,1]{2,1,0:T(8,128)S(1)}, f32[10,18,1]{2,1,0:T(8,128)S(1)}, u32[]{:S(2)}, u32[]{:S(2)}) collective-permute-start(f32[10,18,1]{2,1,0:T(8,128)S(1)} %get-tuple-element.53), channel_id=1, source_target_pairs={{1,0},{3,2},{5,4},{7,6},{9,8},{11,10},{13,12},{15,14},{17,16},{19,... | collective-permute-start | bytes 2168 | tf_op jit(solution)/shard_map/ppermute | solution.py:43
  151.0 7.2 %collective-permute-start.35 = (f32[10,18,1]{2,1,0:T(8,128)S(1)}, f32[10,18,1]{2,1,0:T(8,128)S(1)}, u32[]{:S(2)}, u32[]{:S(2)}) collective-permute-start(f32[10,18,1]{2,1,0:T(8,128)S(1)} %get-tuple-element.52), channel_id=1, source_target_pairs={{0,1},{2,3},{4,5},{6,7},{8,9},{10,11},{12,13},{14,15},{16,17},{18,... | collective-permute-start | bytes 2168 | tf_op jit(solution)/shard_map/ppermute | solution.py:42
  162.1 8.7 %collective-permute-start.36 = (f32[1,16,128]{2,1,0:T(8,128)S(1)}, f32[1,16,128]{2,1,0:T(8,128)S(1)}, u32[]{:S(2)}, u32[]{:S(2)}) collective-permute-start(f32[1,16,128]{2,1,0:T(8,128)S(1)} %get-tuple-element.97), channel_id=1, source_target_pairs={{4,0},{8,4},{12,8},{5,1},{9,5},{13,9},{6,2},{10,6},{14,10},{7,3},{... | collective-permute-start | bytes 24584 | tf_op jit(solution)/shard_map/ppermute | solution.py:43
  163.4 7.4 %collective-permute-start.37 = (f32[1,16,128]{2,1,0:T(8,128)S(1)}, f32[1,16,128]{2,1,0:T(8,128)S(1)}, u32[]{:S(2)}, u32[]{:S(2)}) collective-permute-start(f32[1,16,128]{2,1,0:T(8,128)S(1)} %get-tuple-element.96), channel_id=1, source_target_pairs={{0,4},{4,8},{8,12},{1,5},{5,9},{9,13},{2,6},{6,10},{10,14},{3,7},{... | collective-permute-start | bytes 24584 | tf_op jit(solution)/shard_map/ppermute | solution.py:42
  171.4 6.4 %collective-permute-start.38 = (f32[10,1,128]{2,1,0:T(1,128)S(1)}, f32[10,1,128]{2,1,0:T(1,128)S(1)}, u32[]{:S(2)}, u32[]{:S(2)}) collective-permute-start(f32[10,1,128]{2,1,0:T(1,128)S(1)} %get-tuple-element.77), channel_id=1, source_target_pairs={{2,0},{3,1},{6,4},{7,5},{10,8},{11,9},{14,12},{15,13},{18,16},{19,... | collective-permute-start | bytes 15368 | tf_op jit(solution)/shard_map/ppermute | solution.py:43
  178.9 6.8 %collective-permute-start.40 = (f32[10,18,1]{2,1,0:T(8,128)S(1)}, f32[10,18,1]{2,1,0:T(8,128)S(1)}, u32[]{:S(2)}, u32[]{:S(2)}) collective-permute-start(f32[10,18,1]{2,1,0:T(8,128)S(1)} %get-tuple-element.51), channel_id=1, source_target_pairs={{1,0},{3,2},{5,4},{7,6},{9,8},{11,10},{13,12},{15,14},{17,16},{19,... | collective-permute-start | bytes 2168 | tf_op jit(solution)/shard_map/ppermute | solution.py:43
  180.2 7.0 %collective-permute-start.41 = (f32[10,18,1]{2,1,0:T(8,128)S(1)}, f32[10,18,1]{2,1,0:T(8,128)S(1)}, u32[]{:S(2)}, u32[]{:S(2)}) collective-permute-start(f32[10,18,1]{2,1,0:T(8,128)S(1)} %get-tuple-element.50), channel_id=1, source_target_pairs={{0,1},{2,3},{4,5},{6,7},{8,9},{10,11},{12,13},{14,15},{16,17},{18,... | collective-permute-start | bytes 2168 | tf_op jit(solution)/shard_map/ppermute | solution.py:42
  (149 other events, 2700.4 us)
